TPU v7x, 32 devices: a whole 2x2x4 slice. The times are simulated.
32 devices in a mesh: gx: 8 (over z, core), gy: 4 (over y, x).
Axes of the slice: x: 2, y: 2, z: 4, core: 2. Of those that a mesh axis runs over, the one named last changes fastest.
Arguments:
- tokens: bfloat16 [64, 32, 8, 768], P('gx', 'gy'), may hold values from -64 to 64
- target: bfloat16 [64, 32, 8, 768], P('gx', 'gy'), may hold values from -4 to 4
- norm_gain: float32 [768], replicated, may hold values from 0.1 to 1.9
- qkv_weight: bfloat16 [768, 1152], P('gy'), may hold values from -4 to 4
- proj_weight: bfloat16 [384, 768], P('gy'), may hold values from -1.5 to 1.5
Outputs:
- block_out: bfloat16 [64, 32, 8, 768], P('gx', 'gy')
- qkv_grad: float32 [768, 1152], P('gy')
All inputs are finite; a program needn't handle non-finite values.
Results may differ from a plain program's by a relative error of at most 0.0094.
Values may be sent and summed in bfloat16 or wider, within the bound.
A program may use at most 64 MiB of HBM per device.

v0:
```python
import math
import jax
import jax.numpy as jnp
from jax import lax
from jax.sharding import PartitionSpec as P

HEADS = 12
HD = 32
WIN = 8
norm_eps = 1e-05


def shifted(x, axis, by):
    devices = lax.axis_size(axis)
    return lax.ppermute(x, axis, [(i, (i + by) % devices) for i in range(devices)])


def displace(volume, half_width):
    volume = jnp.roll(volume, -half_width, axis=2)
    upper_rows = shifted(volume[:half_width], "gx", -1)
    volume = jnp.concatenate([volume[half_width:], upper_rows], 0)
    upper_cols = shifted(volume[:, :half_width], "gy", -1)
    return jnp.concatenate([volume[:, half_width:], upper_cols], 1)


def restore(volume, half_width):
    lower_rows = shifted(volume[-half_width:], "gx", 1)
    volume = jnp.concatenate([lower_rows, volume[:-half_width]], 0)
    lower_cols = shifted(volume[:, -half_width:], "gy", 1)
    volume = jnp.concatenate([lower_cols, volume[:, :-half_width]], 1)
    return jnp.roll(volume, half_width, axis=2)


def into_windows(volume, window):
    ext_x, ext_y, ext_z, channels = volume.shape
    blocks = volume.reshape(ext_x, ext_y, ext_z // window, window, channels)
    return blocks.transpose(2, 0, 1, 3, 4).reshape(
        ext_z // window, ext_x * ext_y * window, channels
    )


def from_windows(windows, ext_x, ext_y, window):
    window_count = windows.shape[0]
    channels = windows.shape[2]
    blocks = windows.reshape(window_count, ext_x, ext_y, window, channels).transpose(1, 2, 0, 3, 4)
    return blocks.reshape(ext_x, ext_y, window_count * window, channels)


def head_probs(queries, keys_in, score_scale):
    scores = (
        jnp.einsum("wqd,wkd->wqk", queries, keys_in, preferred_element_type=jnp.float32)
        * score_scale
    )
    row_max = jnp.max(scores, -1, keepdims=True)
    exponent = jnp.exp(scores - row_max)
    return exponent / jnp.sum(exponent, -1, keepdims=True)


def shards(tokens, target, norm_gain, qkv_weight, proj_weight):
    window = WIN
    half_width = WIN // 2
    head_count = HEADS
    head_dim = HD
    inner_dim = HEADS * HD
    score_scale = HD ** (-0.5)
    ext_x, ext_y, ext_z, channels = tokens.shape
    total_tokens = ext_x * ext_y * ext_z * lax.axis_size("gx") * lax.axis_size("gy")
    loss_scale = 2.0 / math.sqrt(total_tokens)
    widened = tokens.astype(jnp.float32)
    token_mean = jnp.mean(widened, -1, keepdims=True)
    centred = widened - token_mean
    variance = jnp.mean(centred * centred, -1, keepdims=True)
    normed = (centred * lax.rsqrt(variance + norm_eps) * norm_gain).astype(jnp.bfloat16)
    windows_in = into_windows(displace(normed, half_width), window)
    window_count = windows_in.shape[0]
    window_tokens = windows_in.shape[1]
    flat_in = windows_in.reshape(-1, channels)
    qkv_whole = lax.all_gather(qkv_weight, "gy", axis=0, tiled=True)
    qkv_act = jnp.dot(flat_in, qkv_whole, preferred_element_type=jnp.float32).astype(jnp.bfloat16)
    qkv_act = qkv_act.reshape(window_count, window_tokens, 3 * inner_dim)

    def forward_head(head_idx, attn_buffer):
        queries = lax.dynamic_slice_in_dim(qkv_act, head_idx * head_dim, head_dim, 2)
        keys_in = lax.dynamic_slice_in_dim(qkv_act, inner_dim + head_idx * head_dim, head_dim, 2)
        values = lax.dynamic_slice_in_dim(qkv_act, 2 * inner_dim + head_idx * head_dim, head_dim, 2)
        attn_prob = head_probs(queries, keys_in, score_scale).astype(jnp.bfloat16)
        mixed = jnp.einsum(
            "wqk,wkd->wqd", attn_prob, values, preferred_element_type=jnp.float32
        ).astype(jnp.bfloat16)
        return lax.dynamic_update_slice_in_dim(attn_buffer, mixed, head_idx * head_dim, 2)

    attn_out = lax.fori_loop(
        0,
        head_count,
        forward_head,
        jnp.zeros((window_count, window_tokens, inner_dim), jnp.bfloat16),
    )
    proj_whole = lax.all_gather(proj_weight, "gy", axis=0, tiled=True)
    contract_cols = (((1,), (1,)), ((), ()))
    block_shift = jnp.dot(
        attn_out.reshape(-1, inner_dim), proj_whole, preferred_element_type=jnp.float32
    ).astype(jnp.bfloat16)
    block_shift = block_shift.reshape(window_count, window_tokens, channels)
    block_out = restore(from_windows(block_shift, ext_x, ext_y, window), half_width)
    grad_out = ((block_out.astype(jnp.float32) - target.astype(jnp.float32)) * loss_scale).astype(
        jnp.bfloat16
    )
    grad_shift = into_windows(displace(grad_out, half_width), window)
    grad_windows = lax.dot_general(
        grad_shift.reshape(-1, channels),
        proj_whole,
        contract_cols,
        preferred_element_type=jnp.float32,
    ).astype(jnp.bfloat16)
    grad_windows = grad_windows.reshape(window_count, window_tokens, inner_dim)

    def backward_head(head_idx, grad_buffer):
        queries = lax.dynamic_slice_in_dim(qkv_act, head_idx * head_dim, head_dim, 2)
        keys_in = lax.dynamic_slice_in_dim(qkv_act, inner_dim + head_idx * head_dim, head_dim, 2)
        values = lax.dynamic_slice_in_dim(qkv_act, 2 * inner_dim + head_idx * head_dim, head_dim, 2)
        attn_prob = head_probs(queries, keys_in, score_scale)
        prob_half = attn_prob.astype(jnp.bfloat16)
        grad_mixed = lax.dynamic_slice_in_dim(grad_windows, head_idx * head_dim, head_dim, 2)
        grad_probs = jnp.einsum(
            "wqd,wkd->wqk", grad_mixed, values, preferred_element_type=jnp.float32
        )
        grad_values = jnp.einsum(
            "wqk,wqd->wkd", prob_half, grad_mixed, preferred_element_type=jnp.float32
        ).astype(jnp.bfloat16)
        row_dot = jnp.sum(grad_probs * attn_prob, -1, keepdims=True)
        grad_scores = (attn_prob * (grad_probs - row_dot)).astype(jnp.bfloat16)
        grad_queries = (
            jnp.einsum("wqk,wkd->wqd", grad_scores, keys_in, preferred_element_type=jnp.float32)
            * score_scale
        ).astype(jnp.bfloat16)
        grad_keys = (
            jnp.einsum("wqk,wqd->wkd", grad_scores, queries, preferred_element_type=jnp.float32)
            * score_scale
        ).astype(jnp.bfloat16)
        grad_buffer = lax.dynamic_update_slice_in_dim(
            grad_buffer, grad_queries, head_idx * head_dim, 2
        )
        grad_buffer = lax.dynamic_update_slice_in_dim(
            grad_buffer, grad_keys, inner_dim + head_idx * head_dim, 2
        )
        return lax.dynamic_update_slice_in_dim(
            grad_buffer, grad_values, 2 * inner_dim + head_idx * head_dim, 2
        )

    grad_qkv = lax.fori_loop(
        0,
        head_count,
        backward_head,
        jnp.zeros((window_count, window_tokens, 3 * inner_dim), jnp.bfloat16),
    )
    grad_flat = grad_qkv.reshape(-1, 3 * inner_dim)
    contract_rows = (((0,), (0,)), ((), ()))
    shard_rows = qkv_weight.shape[0]
    local_grad = lax.dot_general(
        flat_in, grad_flat, contract_rows, preferred_element_type=jnp.float32
    )
    whole_grad = lax.psum(local_grad, ("gx", "gy"))
    qkv_grad = lax.dynamic_slice_in_dim(
        whole_grad, lax.axis_index("gy") * shard_rows, shard_rows, 0
    )
    return (block_out, qkv_grad)


def solution(mesh):
    in_specs = (
        P("gx", "gy", None, None),
        P("gx", "gy", None, None),
        P(),
        P("gy", None),
        P("gy", None),
    )
    out_specs = (P("gx", "gy", None, None), P("gy", None))
    return jax.shard_map(shards, mesh=mesh, in_specs=in_specs, out_specs=out_specs, check_vma=False)
```

profile of v0, /device:TPU:0, one launch (start us, length us, event | category | flops | bytes accessed | tf_op | source)
XLA Modules:
  0.0 313.7 jit_solution(8115496946814767307)
XLA Ops:
  8.0 1.3 convert_reduce_fusion
  10.7 4.6 %collective-permute-start = (bf16[4,8,8,768]{3,2,1,0:T(8,128)(2,1)S(1)}, bf16[4,8,8,768]{3,2,1,0:T(8,128)(2,1)S(1)}, u32[]{:S(2)}, u32[]{:S(2)}) collective-permute-start(bf16[4,8,8,768]{3,2,1,0:T(8,128)(2,1)S(1)} %get-tuple-element.239), channel_id=1, source_target_pairs={{0,28},{4,0},{8,4},{12,8},{16,12},{20,16},{24,20},{28,24},{1,29},{... | collective-permute-start | bytes 1179656 | tf_op jit(solution)/shard_map/ppermute | solution.py:15
  15.3 5.3 %collective-permute-done = bf16[4,8,8,768]{3,2,1,0:T(8,128)(2,1)S(1)} collective-permute-done((bf16[4,8,8,768]{3,2,1,0:T(8,128)(2,1)S(1)}, bf16[4,8,8,768]{3,2,1,0:T(8,128)(2,1)S(1)}, u32[]{:S(2)}, u32[]{:S(2)}) %collective-permute-start) | collective-permute-done | bytes 393248 | tf_op jit(solution)/shard_map/ppermute | solution.py:15
  20.7 2.5 collective-permute-start.1
  23.2 18.8 %all_gather.7 = bf16[384,768]{1,0:T(8,128)(2,1)} all-gather(bf16[96,768]{1,0:T(8,128)(2,1)S(1)} %copy-done.3), channel_id=1, replica_groups=mesh['gx'=8,'gy'=4] {'gy'}, dimensions={0}, use_global_device_ids=true | all-gather | bytes 737280 | tf_op jit(solution)/shard_map/all_gather | solution.py:98
  42.0 13.0 %all-gather.2.cloned.1.call-done = bf16[768,1152]{1,0:T(8,128)(2,1)} async-done(((bf16[192,1152]{1,0:T(8,128)(2,1)}), bf16[768,1152]{1,0:T(8,128)(2,1)}) %all-gather.2.cloned.1.call-update) | async-done | bytes 1769488 | tf_op jit(solution)/shard_map/all_gather | solution.py:78
  55.0 2.7 fusion.43
  57.7 11.2 %while.30 = (s32[]{:T(128)}, bf16[1,512,384]{1,2,0:T(8,128)(2,1)S(1)}, bf16[1,512,1152]{2,1,0:T(8,128)(2,1)S(1)}, s32[]{:T(128)}, s32[]{:T(128)}, /*index=5*/s32...) while((s32[]{:T(128)}, bf16[1,512,384]{1,2,0:T(8,128)(2,1)S(1)}, ...), condition=%wide.region_5.6_spmd, body=%wide.region_2.5_spmd.sunk | while | flops 35404812 | bytes 3582236 | solution.py:92
  68.9 1.7 convolution_convert_fusion.3
  70.7 9.0 %collective-permute-done.2 = bf16[4,8,8,768]{3,2,1,0:T(8,128)(2,1)S(1)} collective-permute-done((bf16[4,8,8,768]{3,2,1,0:T(8,128)(2,1)S(1)}, bf16[4,8,8,768]{3,2,1,0:T(8,128)(2,1)S(1)}, u32[]{:S(2)}, u32[]{:S(2)}) %collective-permute-start.2) | collective-permute-done | bytes 393248 | tf_op jit(solution)/shard_map/ppermute | solution.py:15
  79.7 1.5 collective-permute-start.3
  81.3 7.8 %collective-permute-done.3 = bf16[8,4,8,768]{3,2,1,0:T(8,128)(2,1)S(1)} collective-permute-done((bf16[8,4,8,768]{3,2,1,0:T(8,128)(2,1)S(1)}, bf16[8,4,8,768]{3,2,1,0:T(8,128)(2,1)S(1)}, u32[]{:S(2)}, u32[]{:S(2)}) %collective-permute-start.3) | collective-permute-done | bytes 393248 | tf_op jit(solution)/shard_map/ppermute | solution.py:15
  90.3 1.5 multiply_convert_fusion.1
  92.5 5.3 %collective-permute-done.4 = bf16[4,8,8,768]{3,2,1,0:T(8,128)(2,1)S(1)} collective-permute-done((bf16[4,8,8,768]{3,2,1,0:T(8,128)(2,1)S(1)}, bf16[4,8,8,768]{3,2,1,0:T(8,128)(2,1)S(1)}, u32[]{:S(2)}, u32[]{:S(2)}) %collective-permute-start.4) | collective-permute-done | bytes 393248 | tf_op jit(solution)/shard_map/ppermute | solution.py:15
  98.5 10.7 %collective-permute-done.5 = bf16[8,4,8,768]{3,2,1,0:T(8,128)(2,1)} collective-permute-done((bf16[8,4,8,768]{3,2,1,0:T(8,128)(2,1)S(1)}, bf16[8,4,8,768]{3,2,1,0:T(8,128)(2,1)}, u32[]{:S(2)}, u32[]{:S(2)}) %collective-permute-start.5) | collective-permute-done | bytes 393248 | tf_op jit(solution)/shard_map/ppermute | solution.py:15
  109.2 1.1 pad_maximum_fusion.3
  110.9 1.1 broadcast_in_dim.25
  112.0 49.0 %while.31 = (s32[]{:T(128)}, bf16[1,512,1152]{1,2,0:T(8,128)(2,1)}, bf16[1,512,1152]{2,1,0:T(8,128)(2,1)S(1)}, bf16[1,512,384]{2,1,0:T(8,128)(2,1)S(1)}, s32[]{:...) while((s32[]{:T(128)}, bf16[1,512,1152]{1,2,0:T(8,128)(2,1)}, ...), condition=%wide.region_10.11_spmd, body=%wide.region_6.10_spmd.sunk | while | flops 88160776 | bytes 9951548 | solution.py:150
  134.6 1.0 fusion.101
  151.0 0.9 fusion.101
  159.1 0.9 fusion.101
  161.0 4.2 %fusion.50 = f32[768,1152]{1,0:T(8,128)} fusion(bf16[512,768]{1,0:T(8,128)(2,1)S(1)} %bitcast.110, bf16[1,512,1152]{1,2,0:T(8,128)(2,1)} %get-tuple-element.203), kind=kOutput, calls=%fused_computation.66 | convolution fusion | flops 905969664 | bytes 5505024 | tf_op jit(solution)/shard_map/dot_general | solution.py:159
  165.3 139.4 %all-reduce.2.cloned.1.call-done = f32[768,1152]{1,0:T(8,128)} async-done(((f32[768,1152]{1,0:T(8,128)}), f32[768,1152]{1,0:T(8,128)}) %all-reduce.2.cloned.1.call-update) | async-done | bytes 3538960 | tf_op jit(solution)/shard_map/psum | solution.py:162
  304.7 2.1 constant_dynamic-slice_fusion
  (152 shorter events, 62.7 us)
Async XLA Ops:
  7.2 2.1 copy-start
  7.2 2.5 copy-start.4
  7.2 47.9 %all-gather.2.cloned.1.call-start = ((), (), s32[]{:S(2)}) async-start(), calls=%async_computation | async-start | bytes 2211840 | tf_op jit(solution)/shard_map/all_gather | solution.py:78
  7.9 296.8 %all-reduce.2.cloned.1.call-start = ((), (), s32[]{:S(2)}) async-start(), calls=%async_computation.1 | async-start | bytes 7077888 | tf_op jit(solution)/shard_map/psum | solution.py:162
  10.7 12.5 %copy-start.3 = (bf16[96,768]{1,0:T(8,128)(2,1)S(1)}, bf16[96,768]{1,0:T(8,128)(2,1)}, u32[]{:S(2)}) copy-start(bf16[96,768]{1,0:T(8,128)(2,1)} %param.13) | copy-start | bytes 442372
  10.7 9.9 %collective-permute-start = (bf16[4,8,8,768]{3,2,1,0:T(8,128)(2,1)S(1)}, bf16[4,8,8,768]{3,2,1,0:T(8,128)(2,1)S(1)}, u32[]{:S(2)}, u32[]{:S(2)}) collective-permute-start(bf16[4,8,8,768]{3,2,1,0:T(8,128)(2,1)S(1)} %get-tuple-element.239), channel_id=1, source_target_pairs={{0,28},{4,0},{8,4},{12,8},{16,12},{20,16},{24,20},{28,24},{1,29},{... | collective-permute-start | bytes 1179656 | tf_op jit(solution)/shard_map/ppermute | solution.py:15
  20.7 21.3 %collective-permute-start.1 = (bf16[8,4,8,768]{3,2,1,0:T(8,128)(2,1)S(1)}, bf16[8,4,8,768]{3,2,1,0:T(8,128)(2,1)S(1)}, u32[]{:S(2)}, u32[]{:S(2)}) collective-permute-start(bf16[8,4,8,768]{3,2,1,0:T(8,128)(2,1)S(1)} %get-tuple-element.237), channel_id=1, source_target_pairs={{0,3},{1,0},{2,1},{3,2},{4,7},{5,4},{6,5},{7,6},{8,11},{9,8},{10,9... | collective-permute-start | bytes 1179656 | tf_op jit(solution)/shard_map/ppermute | solution.py:15
  70.7 9.1 %collective-permute-start.2 = (bf16[4,8,8,768]{3,2,1,0:T(8,128)(2,1)S(1)}, bf16[4,8,8,768]{3,2,1,0:T(8,128)(2,1)S(1)}, u32[]{:S(2)}, u32[]{:S(2)}) collective-permute-start(bf16[4,8,8,768]{3,2,1,0:T(8,128)(2,1)S(1)} %bitcast.114), channel_id=1, source_target_pairs={{0,4},{4,8},{8,12},{12,16},{16,20},{20,24},{24,28},{28,0},{1,5},{5... | collective-permute-start | bytes 1179656 | tf_op jit(solution)/shard_map/ppermute | solution.py:15
  79.7 9.3 %collective-permute-start.3 = (bf16[8,4,8,768]{3,2,1,0:T(8,128)(2,1)S(1)}, bf16[8,4,8,768]{3,2,1,0:T(8,128)(2,1)S(1)}, u32[]{:S(2)}, u32[]{:S(2)}) collective-permute-start(bf16[8,4,8,768]{3,2,1,0:T(8,128)(2,1)S(1)} %fusion.55), channel_id=1, source_target_pairs={{0,1},{1,2},{2,3},{3,0},{4,5},{5,6},{6,7},{7,4},{8,9},{9,10},{10,1... | collective-permute-start | bytes 1179656 | tf_op jit(solution)/shard_map/ppermute | solution.py:15
  89.1 1.1 copy-start.2
  92.5 5.4 %collective-permute-start.4 = (bf16[4,8,8,768]{3,2,1,0:T(8,128)(2,1)S(1)}, bf16[4,8,8,768]{3,2,1,0:T(8,128)(2,1)S(1)}, u32[]{:S(2)}, u32[]{:S(2)}) collective-permute-start(bf16[4,8,8,768]{3,2,1,0:T(8,128)(2,1)S(1)} %get-tuple-element.229), channel_id=1, source_target_pairs={{0,28},{4,0},{8,4},{12,8},{16,12},{20,16},{24,20},{28,24},{1,29},{... | collective-permute-start | bytes 1179656 | tf_op jit(solution)/shard_map/ppermute | solution.py:15
  97.9 12.4 %copy-start.1 = (bf16[384,768]{1,0:T(8,128)(2,1)S(1)}, bf16[384,768]{1,0:T(8,128)(2,1)}, u32[]{:S(2)}) copy-start(bf16[384,768]{1,0:T(8,128)(2,1)} %all_gather.7) | copy-start | bytes 1769476
  97.9 11.4 %collective-permute-start.5 = (bf16[8,4,8,768]{3,2,1,0:T(8,128)(2,1)S(1)}, bf16[8,4,8,768]{3,2,1,0:T(8,128)(2,1)}, u32[]{:S(2)}, u32[]{:S(2)}) collective-permute-start(bf16[8,4,8,768]{3,2,1,0:T(8,128)(2,1)S(1)} %get-tuple-element.227), channel_id=1, source_target_pairs={{0,3},{1,0},{2,1},{3,2},{4,7},{5,4},{6,5},{7,6},{8,11},{9,8},{10,9... | collective-permute-start | bytes 1179656 | tf_op jit(solution)/shard_map/ppermute | solution.py:15
Sparse Core Ops, SparseCore 0:
  9.8 45.1 all-gather.1
  165.4 139.2 all-reduce.1
where the time goes:
time: 314 us
  waiting for transfers between devices  191 us (61%)
  matrix products  60.9 us (19%)
  blocking collectives  18.8 us (6%)
  between operations  14.3 us (5%)
  other arithmetic  13.7 us (4%)
  starting transfers between devices  9.39 us (3%)
  local copies, waits for them, and re-layouts  5.15 us (2%)
    psum x1, waiting for transfers between devices, shards(): whole_grad = lax.psum(local_grad, ('gx', 'gy'))  139 us
    ppermute x6, waiting for transfers between devices, shifted(): lax.ppermute(x, axis, [(i, (i + by) % devices) for i in range(devices)])  38.1 us
    all_gather x1, blocking collectives, shards(): proj_whole = lax.all_gather(proj_weight, 'gy', axis=0, tiled=True)  18.8 us
    all_gather x1, waiting for transfers between devices, shards(): qkv_whole = lax.all_gather(qkv_weight, 'gy', axis=0, tiled=True)  13 us
    dot_general x12, matrix products, backward_head(): jnp.einsum('wqk,wqd->wkd', grad_scores, queries, preferred_element_type=j...  11.3 us
    dot_general x12, matrix products, backward_head(): jnp.einsum('wqk,wqd->wkd', prob_half, grad_mixed, preferred_element_type=...  11.2 us
    dot_general x12, matrix products, backward_head(): jnp.einsum('wqk,wkd->wqd', grad_scores, keys_in, preferred_element_type=j...  11 us
    dot_general x24, matrix products, head_probs(): jnp.einsum('wqd,wkd->wqk', queries, keys_in, preferred_element_type=jnp.f...  9.39 us
  transfers between devices with their start and end apart: 8, of which 7 were waited for; matrix products, arithmetic and copies ran while one was open for 1% of the time, Pallas kernels for 0%

commit v1 on v0

--- a/solution.py
+++ b/solution.py
@@ -95,7 +95,24 @@
         forward_head,
         jnp.zeros((window_count, window_tokens, inner_dim), jnp.bfloat16),
     )
-    proj_whole = lax.all_gather(proj_weight, "gy", axis=0, tiled=True)
+    size, index, rows = (lax.axis_size("gy"), lax.axis_index("gy"), proj_weight.shape[0])
+    ahead = [(i_2, (i_2 + 1) % size) for i_2 in range(size)]
+    left = [(i_2, (i_2 - 1) % size) for i_2 in range(size)]
+    out = jnp.zeros(
+        (*proj_weight.shape[:0], size * rows, *proj_weight.shape[0 + 1 :]), proj_weight.dtype
+    )
+    out = lax.dynamic_update_slice_in_dim(out, proj_weight, index * rows, axis=0)
+    from_left = from_right = proj_weight
+    half = size // 2
+    for lap in range(1, half + 1):
+        from_left = lax.ppermute(from_left, "gy", ahead)
+        out = lax.dynamic_update_slice_in_dim(out, from_left, (index - lap) % size * rows, axis=0)
+        if lap < size - half:
+            from_right = lax.ppermute(from_right, "gy", left)
+            out = lax.dynamic_update_slice_in_dim(
+                out, from_right, (index + lap) % size * rows, axis=0
+            )
+    proj_whole = out
     contract_cols = (((1,), (1,)), ((), ()))
     block_shift = jnp.dot(
         attn_out.reshape(-1, inner_dim), proj_whole, preferred_element_type=jnp.float32

time: 314 us -> 287 us (0.914)
  matrix products: 60.9 us -> 37.1 us
  blocking collectives: 18.8 us -> 0 us
  waiting for transfers between devices: 191 us -> 203 us
  starting transfers between devices: 9.39 us -> 14.3 us
    all_gather x1 -> x0, blocking collectives: 18.8 us -> none  [shards(): proj_whole = lax.all_gather(proj_weight, 'gy', axis=0, tiled=True)]
    ppermute x0 -> x3, waiting for transfers between devices: none -> 14.3 us  [the longest x2 14.3 us: shards(): from_left = lax.ppermute(from_left, 'gy', ahead)]
    dot_general x12, matrix products: 11 us -> 3.62 us  [backward_head(): jnp.einsum('wqk,wkd->wqd', grad_scores, keys_in, preferred_element_type=j...]
    dot_general x12, matrix products: 11.3 us -> 3.94 us  [backward_head(): jnp.einsum('wqk,wqd->wkd', grad_scores, queries, preferred_element_type=j...]
    dot_general x12, matrix products: 11.2 us -> 4.18 us  [backward_head(): jnp.einsum('wqk,wqd->wkd', prob_half, grad_mixed, preferred_element_type=...]
    ppermute x0 -> x3, starting transfers between devices: none -> 4.93 us  [the longest x2 2.48 us: shards(): from_left = lax.ppermute(from_left, 'gy', ahead)]
  transfers between devices with their start and end apart: 8 -> 11, of which waited for: 7 -> 9; matrix products, arithmetic and copies ran while one was open for 1% -> 1% of each run, Pallas kernels for 0% -> 0%
where the time goes in v1:
time: 287 us
  waiting for transfers between devices  203 us (71%)
  matrix products  37.1 us (13%)
  starting transfers between devices  14.3 us (5%)
  between operations  14.3 us (5%)
  other arithmetic  13.7 us (5%)
  local copies, waits for them, and re-layouts  4.22 us (1%)
    psum x1, waiting for transfers between devices, shards(): whole_grad = lax.psum(local_grad, ('gx', 'gy'))  139 us
    ppermute x6, waiting for transfers between devices, shifted(): lax.ppermute(x, axis, [(i, (i + by) % devices) for i in range(devices)])  35.6 us
    ppermute x2, waiting for transfers between devices, shards(): from_left = lax.ppermute(from_left, 'gy', ahead)  14.3 us
    all_gather x1, waiting for transfers between devices, shards(): qkv_whole = lax.all_gather(qkv_weight, 'gy', axis=0, tiled=True)  12.7 us
    dot_general x24, matrix products, head_probs(): jnp.einsum('wqd,wkd->wqk', queries, keys_in, preferred_element_type=jnp.f...  9.61 us
    ppermute x6, starting transfers between devices, shifted(): lax.ppermute(x, axis, [(i, (i + by) % devices) for i in range(devices)])  9.31 us
  transfers between devices with their start and end apart: 11, of which 9 were waited for; matrix products, arithmetic and copies ran while one was open for 1% of the time, Pallas kernels for 0%

profile of v1, /device:TPU:0, one launch (start us, length us, event | category | flops | bytes accessed | tf_op | source)
XLA Modules:
  0.0 286.5 jit_solution(16184020242296857866)
XLA Ops:
  7.2 0.7 all-gather.2.cloned.1.call-update
  8.0 1.3 convert_reduce_fusion
  10.7 4.6 %collective-permute-start = (bf16[4,8,8,768]{3,2,1,0:T(8,128)(2,1)S(1)}, bf16[4,8,8,768]{3,2,1,0:T(8,128)(2,1)S(1)}, u32[]{:S(2)}, u32[]{:S(2)}) collective-permute-start(bf16[4,8,8,768]{3,2,1,0:T(8,128)(2,1)S(1)} %get-tuple-element.239), channel_id=1, source_target_pairs={{0,28},{4,0},{8,4},{12,8},{16,12},{20,16},{24,20},{28,24},{1,29},{... | collective-permute-start | bytes 1179656 | tf_op jit(solution)/shard_map/ppermute | solution.py:15
  15.3 2.4 collective-permute-start.3
  17.8 2.8 collective-permute-done
  20.7 2.5 collective-permute-start.1
  23.3 2.4 collective-permute-done.2
  25.7 2.5 collective-permute-start.4
  28.2 11.9 %collective-permute-done.4 = bf16[96,768]{1,0:T(8,128)(2,1)S(1)} collective-permute-done((bf16[96,768]{1,0:T(8,128)(2,1)S(1)}, bf16[96,768]{1,0:T(8,128)(2,1)S(1)}, u32[]{:S(2)}, u32[]{:S(2)}) %collective-permute-start.4) | collective-permute-done | bytes 147488 | tf_op jit(solution)/shard_map/ppermute | solution.py:108
  40.2 12.7 %all-gather.2.cloned.1.call-done = bf16[768,1152]{1,0:T(8,128)(2,1)} async-done(((bf16[192,1152]{1,0:T(8,128)(2,1)}), bf16[768,1152]{1,0:T(8,128)(2,1)}) %all-gather.2.cloned.1.call-update) | async-done | bytes 1769488 | tf_op jit(solution)/shard_map/all_gather | solution.py:78
  52.9 2.7 fusion.43
  55.6 11.1 %while.30 = (s32[]{:T(128)}, bf16[1,512,384]{1,2,0:T(8,128)(2,1)S(1)}, bf16[1,512,1152]{2,1,0:T(8,128)(2,1)S(1)}, s32[]{:T(128)}, s32[]{:T(128)}, /*index=5*/s32...) while((s32[]{:T(128)}, bf16[1,512,384]{1,2,0:T(8,128)(2,1)S(1)}, ...), condition=%wide.region_5.6_spmd, body=%wide.region_2.5_spmd.sunk | while | flops 35404812 | bytes 3582228 | solution.py:92
  67.4 9.0 %collective-permute-done.5 = bf16[4,8,8,768]{3,2,1,0:T(8,128)(2,1)S(1)} collective-permute-done((bf16[4,8,8,768]{3,2,1,0:T(8,128)(2,1)S(1)}, bf16[4,8,8,768]{3,2,1,0:T(8,128)(2,1)S(1)}, u32[]{:S(2)}, u32[]{:S(2)}) %collective-permute-start.5) | collective-permute-done | bytes 393248 | tf_op jit(solution)/shard_map/ppermute | solution.py:15
  76.5 1.5 collective-permute-start.6
  78.0 7.8 %collective-permute-done.6 = bf16[8,4,8,768]{3,2,1,0:T(8,128)(2,1)S(1)} collective-permute-done((bf16[8,4,8,768]{3,2,1,0:T(8,128)(2,1)S(1)}, bf16[8,4,8,768]{3,2,1,0:T(8,128)(2,1)S(1)}, u32[]{:S(2)}, u32[]{:S(2)}) %collective-permute-start.6) | collective-permute-done | bytes 393248 | tf_op jit(solution)/shard_map/ppermute | solution.py:15
  86.2 0.8 copy-done.1
  87.0 1.5 multiply_convert_fusion.1
  89.2 5.3 %collective-permute-done.7 = bf16[4,8,8,768]{3,2,1,0:T(8,128)(2,1)S(1)} collective-permute-done((bf16[4,8,8,768]{3,2,1,0:T(8,128)(2,1)S(1)}, bf16[4,8,8,768]{3,2,1,0:T(8,128)(2,1)S(1)}, u32[]{:S(2)}, u32[]{:S(2)}) %collective-permute-start.7) | collective-permute-done | bytes 393248 | tf_op jit(solution)/shard_map/ppermute | solution.py:15
  95.2 10.7 %collective-permute-done.8 = bf16[8,4,8,768]{3,2,1,0:T(8,128)(2,1)} collective-permute-done((bf16[8,4,8,768]{3,2,1,0:T(8,128)(2,1)S(1)}, bf16[8,4,8,768]{3,2,1,0:T(8,128)(2,1)}, u32[]{:S(2)}, u32[]{:S(2)}) %collective-permute-start.8) | collective-permute-done | bytes 393248 | tf_op jit(solution)/shard_map/ppermute | solution.py:15
  105.9 1.1 pad_maximum_fusion.3
  107.7 27.5 %while.31 = (s32[]{:T(128)}, bf16[1,512,1152]{1,2,0:T(8,128)(2,1)S(1)}, bf16[1,512,1152]{2,1,0:T(8,128)(2,1)S(1)}, bf16[1,512,384]{2,1,0:T(8,128)(2,1)S(1)}, s32...) while((s32[]{:T(128)}, ...), condition=%wide.region_10.11_spmd, body=%wide.region_6.10_spmd.sunk | while | flops 88160776 | bytes 9951540 | solution.py:167
  135.2 3.0 %fusion.50 = f32[768,1152]{1,0:T(8,128)} fusion(bf16[512,768]{1,0:T(8,128)(2,1)S(1)} %bitcast.110, bf16[1,512,1152]{1,2,0:T(8,128)(2,1)S(1)} %get-tuple-element.203), kind=kOutput, calls=%fused_computation.66 | convolution fusion | flops 905969664 | bytes 5505024 | tf_op jit(solution)/shard_map/dot_general | solution.py:176
  138.2 139.3 %all-reduce.2.cloned.1.call-done = f32[768,1152]{1,0:T(8,128)} async-done(((f32[768,1152]{1,0:T(8,128)}), f32[768,1152]{1,0:T(8,128)}) %all-reduce.2.cloned.1.call-update) | async-done | bytes 3538960 | tf_op jit(solution)/shard_map/psum | solution.py:179
  277.5 2.1 constant_dynamic-slice_fusion
  (160 shorter events, 43.4 us)
Async XLA Ops:
  7.2 2.1 copy-start
  7.2 2.5 copy-start.3
  7.2 45.7 %all-gather.2.cloned.1.call-start = ((), (), s32[]{:S(2)}) async-start(), calls=%async_computation | async-start | bytes 2211840 | tf_op jit(solution)/shard_map/all_gather | solution.py:78
  7.9 269.6 %all-reduce.2.cloned.1.call-start = ((), (), s32[]{:S(2)}) async-start(), calls=%async_computation.1 | async-start | bytes 7077888 | tf_op jit(solution)/shard_map/psum | solution.py:179
  10.3 5.0 %copy-start.2 = (bf16[96,768]{1,0:T(8,128)(2,1)S(1)}, bf16[96,768]{1,0:T(8,128)(2,1)}, u32[]{:S(2)}) copy-start(bf16[96,768]{1,0:T(8,128)(2,1)} %param.13) | copy-start | bytes 442372
  10.7 9.9 %collective-permute-start = (bf16[4,8,8,768]{3,2,1,0:T(8,128)(2,1)S(1)}, bf16[4,8,8,768]{3,2,1,0:T(8,128)(2,1)S(1)}, u32[]{:S(2)}, u32[]{:S(2)}) collective-permute-start(bf16[4,8,8,768]{3,2,1,0:T(8,128)(2,1)S(1)} %get-tuple-element.239), channel_id=1, source_target_pairs={{0,28},{4,0},{8,4},{12,8},{16,12},{20,16},{24,20},{28,24},{1,29},{... | collective-permute-start | bytes 1179656 | tf_op jit(solution)/shard_map/ppermute | solution.py:15
  15.3 12.9 %collective-permute-start.3 = (bf16[96,768]{1,0:T(8,128)(2,1)S(1)}, bf16[96,768]{1,0:T(8,128)(2,1)S(1)}, u32[]{:S(2)}, u32[]{:S(2)}) collective-permute-start(bf16[96,768]{1,0:T(8,128)(2,1)S(1)} %copy-done.2), channel_id=1, source_target_pairs={{0,3},{1,0},{2,1},{3,2},{4,7},{5,4},{6,5},{7,6},{8,11},{9,8},{10,9... | collective-permute-start | bytes 442376 | tf_op jit(solution)/shard_map/ppermute | solution.py:111
  17.8 7.9 %collective-permute-start.2 = (bf16[96,768]{1,0:T(8,128)(2,1)S(1)}, bf16[96,768]{1,0:T(8,128)(2,1)S(1)}, u32[]{:S(2)}, u32[]{:S(2)}) collective-permute-start(bf16[96,768]{1,0:T(8,128)(2,1)S(1)} %copy-done.2), channel_id=1, source_target_pairs={{0,1},{1,2},{2,3},{3,0},{4,5},{5,6},{6,7},{7,4},{8,9},{9,10},{10,1... | collective-permute-start | bytes 442376 | tf_op jit(solution)/shard_map/ppermute | solution.py:108
  20.7 19.5 %collective-permute-start.1 = (bf16[8,4,8,768]{3,2,1,0:T(8,128)(2,1)S(1)}, bf16[8,4,8,768]{3,2,1,0:T(8,128)(2,1)S(1)}, u32[]{:S(2)}, u32[]{:S(2)}) collective-permute-start(bf16[8,4,8,768]{3,2,1,0:T(8,128)(2,1)S(1)} %get-tuple-element.237), channel_id=1, source_target_pairs={{0,3},{1,0},{2,1},{3,2},{4,7},{5,4},{6,5},{7,6},{8,11},{9,8},{10,9... | collective-permute-start | bytes 1179656 | tf_op jit(solution)/shard_map/ppermute | solution.py:15
  25.7 14.4 %collective-permute-start.4 = (bf16[96,768]{1,0:T(8,128)(2,1)S(1)}, bf16[96,768]{1,0:T(8,128)(2,1)S(1)}, u32[]{:S(2)}, u32[]{:S(2)}) collective-permute-start(bf16[96,768]{1,0:T(8,128)(2,1)S(1)} %collective-permute-done.2), channel_id=1, source_target_pairs={{0,1},{1,2},{2,3},{3,0},{4,5},{5,6},{6,7},{7,4},{8,9},{9,10},{10,1... | collective-permute-start | bytes 442376 | tf_op jit(solution)/shard_map/ppermute | solution.py:108
  67.4 9.1 %collective-permute-start.5 = (bf16[4,8,8,768]{3,2,1,0:T(8,128)(2,1)S(1)}, bf16[4,8,8,768]{3,2,1,0:T(8,128)(2,1)S(1)}, u32[]{:S(2)}, u32[]{:S(2)}) collective-permute-start(bf16[4,8,8,768]{3,2,1,0:T(8,128)(2,1)S(1)} %bitcast.114), channel_id=1, source_target_pairs={{0,4},{4,8},{8,12},{12,16},{16,20},{20,24},{24,28},{28,0},{1,5},{5... | collective-permute-start | bytes 1179656 | tf_op jit(solution)/shard_map/ppermute | solution.py:15
  76.5 9.3 %collective-permute-start.6 = (bf16[8,4,8,768]{3,2,1,0:T(8,128)(2,1)S(1)}, bf16[8,4,8,768]{3,2,1,0:T(8,128)(2,1)S(1)}, u32[]{:S(2)}, u32[]{:S(2)}) collective-permute-start(bf16[8,4,8,768]{3,2,1,0:T(8,128)(2,1)S(1)} %fusion.55), channel_id=1, source_target_pairs={{0,1},{1,2},{2,3},{3,0},{4,5},{5,6},{6,7},{7,4},{8,9},{9,10},{10,1... | collective-permute-start | bytes 1179656 | tf_op jit(solution)/shard_map/ppermute | solution.py:15
  85.8 1.1 copy-start.1
  89.2 5.4 %collective-permute-start.7 = (bf16[4,8,8,768]{3,2,1,0:T(8,128)(2,1)S(1)}, bf16[4,8,8,768]{3,2,1,0:T(8,128)(2,1)S(1)}, u32[]{:S(2)}, u32[]{:S(2)}) collective-permute-start(bf16[4,8,8,768]{3,2,1,0:T(8,128)(2,1)S(1)} %get-tuple-element.229), channel_id=1, source_target_pairs={{0,28},{4,0},{8,4},{12,8},{16,12},{20,16},{24,20},{28,24},{1,29},{... | collective-permute-start | bytes 1179656 | tf_op jit(solution)/shard_map/ppermute | solution.py:15
  94.6 11.3 %collective-permute-start.8 = (bf16[8,4,8,768]{3,2,1,0:T(8,128)(2,1)S(1)}, bf16[8,4,8,768]{3,2,1,0:T(8,128)(2,1)}, u32[]{:S(2)}, u32[]{:S(2)}) collective-permute-start(bf16[8,4,8,768]{3,2,1,0:T(8,128)(2,1)S(1)} %get-tuple-element.227), channel_id=1, source_target_pairs={{0,3},{1,0},{2,1},{3,2},{4,7},{5,4},{6,5},{7,6},{8,11},{9,8},{10,9... | collective-permute-start | bytes 1179656 | tf_op jit(solution)/shard_map/ppermute | solution.py:15
Sparse Core Ops, SparseCore 0:
  9.8 43.0 all-gather.1
  138.4 139.1 all-reduce.1
